TPU v7x, 32 devices: a whole 2x2x4 slice. The times are simulated.
32 devices in a mesh: blk: 8 (over z, x), table: 4 (over y, core).
Axes of the slice: x: 2, y: 2, z: 4, core: 2. Of those that a mesh axis runs over, the one named last changes fastest.
Arguments:
- hot_slab: bfloat16 [128, 128], P('blk'), may hold values from -1.5 to 1.5
- hot_ids: int32 [4096, 16], P(('blk', 'table')), may hold values from 0 to 127
- dense: bfloat16 [4096, 128], P(('blk', 'table')), may hold values from -6 to 6
- cold_ids: int32 [4096, 26], P(('blk', 'table')), may hold values from 0 to 511
- table_slot: int32 [26], replicated, may hold values from 0 to 27, as said below
- cold_tables: bfloat16 [28, 512, 128], P('table'), may hold values from -6 to 6
- down_rank: bfloat16 [3456, 512], replicated, may hold values from -0.109375 to 0.109375
- up_rank: bfloat16 [512, 3456], replicated, may hold values from -0.25 to 0.25
- cross_bias: float32 [3456], replicated, may hold values from -3 to 3
- cotangent: bfloat16 [4096, 3456], P(('blk', 'table')), may hold values from -6 to 6
Outputs:
- crossed: bfloat16 [4096, 3456], P(('blk', 'table'))
- table_grad: float32 [8, 28, 512, 128], P('blk', 'table')
Inputs may be any that keep to these rules, and one draw needn't show every extreme that they name: `table_slot`: distinct values; some owner has all 7 of its slots taken.
All inputs are finite; a program needn't handle non-finite values.
Results may differ from a plain program's by a relative error of at most 0.0052.
Values may be sent and summed in bfloat16 or wider, within the bound.
No kernel may reach another device: no remote copies, remote signals or barrier semaphores. Data moves between devices by JAX's collectives and lax.ppermute only.
A program may use at most 64 MiB of HBM per device.

v0:
```python
import jax
import jax.numpy as jnp
from jax import lax
from jax.sharding import PartitionSpec as P


def bag_counts(row_ids, width_rows):
    positions = lax.broadcasted_iota(jnp.int32, (row_ids.shape[0], width_rows), 1)
    counts = jnp.zeros((row_ids.shape[0], width_rows), jnp.float32)
    for bag_index in range(row_ids.shape[1]):
        local_ids = row_ids[:, bag_index : bag_index + 1]
        counts = counts + (local_ids == positions).astype(jnp.float32)
    return counts.astype(jnp.bfloat16)


def on_device(
    hot_slab,
    hot_ids,
    dense,
    cold_ids,
    table_slot,
    cold_tables,
    down_rank,
    up_rank,
    cross_bias,
    cotangent,
):
    batch_rows = dense.shape[0]
    width = hot_slab.shape[1]
    table_count = table_slot.shape[0]
    owners = lax.axis_size("table")
    slots = cold_tables.shape[0]
    table_rows = cold_tables.shape[1]
    slot_total = owners * slots
    block_rows = lax.all_gather(hot_slab, "blk", axis=0, tiled=True)
    counts = bag_counts(hot_ids, block_rows.shape[0])
    pooled = jnp.dot(counts, block_rows, preferred_element_type=jnp.float32)
    front_row = (dense.astype(jnp.float32) + pooled).astype(jnp.bfloat16)
    slot_match = (
        table_slot[:, None] == lax.broadcasted_iota(jnp.int32, (table_count, slot_total), 1)
    ).astype(jnp.int32)
    send_ids = jnp.sum(cold_ids[:, :, None] * slot_match[None, :, :], axis=1).reshape(
        batch_rows, owners, slots
    )
    ids_block = lax.all_to_all(send_ids, "table", split_axis=1, concat_axis=1, tiled=True)
    item_count = ids_block.shape[0]
    row_count = item_count * ids_block.shape[1]
    columns = lax.broadcasted_iota(jnp.int32, (row_count, table_rows), 1)
    pieces = []
    for lookup_slot_index in range(slots):
        lookup_slot_ids = ids_block[:, :, lookup_slot_index].reshape(row_count, 1)
        lookup_selector = (lookup_slot_ids == columns).astype(jnp.bfloat16)
        rows_out = jnp.dot(
            lookup_selector, cold_tables[lookup_slot_index], preferred_element_type=jnp.float32
        )
        pieces.append(rows_out.astype(jnp.bfloat16).reshape(item_count, ids_block.shape[1], width))
    fetched_rows = jnp.stack(pieces, axis=2)
    returned = lax.all_to_all(fetched_rows, "table", split_axis=1, concat_axis=1, tiled=True)
    slot_pick = slot_match.astype(jnp.bfloat16)
    cold_rows = jnp.einsum(
        "skd,tk->std",
        returned.reshape(batch_rows, slot_total, width),
        slot_pick,
        preferred_element_type=jnp.float32,
    ).astype(jnp.bfloat16)
    feat_count = (table_count + 1) * width
    features = jnp.concatenate([front_row[:, None, :], cold_rows], axis=1).reshape(
        batch_rows, feat_count
    )
    low_rank = jnp.dot(features, down_rank, preferred_element_type=jnp.float32).astype(jnp.bfloat16)
    gate = jnp.dot(low_rank, up_rank, preferred_element_type=jnp.float32) + cross_bias[None, :]
    feat_wide = features.astype(jnp.float32)
    crossed = (feat_wide * gate + feat_wide).astype(jnp.bfloat16)
    cot_wide = cotangent.astype(jnp.float32)
    mixed = (cot_wide * feat_wide).astype(jnp.bfloat16)
    grad_low = jnp.dot(mixed, up_rank.T, preferred_element_type=jnp.float32).astype(jnp.bfloat16)
    grad_in = cot_wide * (gate + 1.0) + jnp.dot(
        grad_low, down_rank.T, preferred_element_type=jnp.float32
    )
    grad_in = grad_in.astype(jnp.bfloat16)
    grad_cold = grad_in.reshape(batch_rows, table_count + 1, width)[:, 1:, :]
    grad_slots = jnp.einsum("std,tk->skd", grad_cold, slot_pick, preferred_element_type=jnp.float32)
    grad_slots = grad_slots.astype(jnp.bfloat16).reshape(batch_rows, owners, slots, width)
    arrived = lax.all_to_all(grad_slots, "table", split_axis=1, concat_axis=1, tiled=True)
    row_positions = lax.broadcasted_iota(jnp.int32, (table_rows, batch_rows * owners), 0)
    slot_grads = []
    for slot_index in range(slots):
        slot_ids = ids_block[:, :, slot_index].reshape(1, batch_rows * owners)
        slot_rows = arrived[:, :, slot_index, :].reshape(batch_rows * owners, width)
        selector = (row_positions == slot_ids).astype(jnp.bfloat16)
        slot_grads.append(jnp.dot(selector, slot_rows, preferred_element_type=jnp.float32))
    table_grad = jnp.stack(slot_grads, axis=0)[None]
    return (crossed, table_grad)


def solution(mesh):
    placed = (
        P("blk", None),
        P(("blk", "table"), None),
        P(("blk", "table"), None),
        P(("blk", "table"), None),
        P(),
        P("table", None, None),
        P(),
        P(),
        P(),
        P(("blk", "table"), None),
    )
    return jax.shard_map(
        on_device,
        mesh=mesh,
        in_specs=placed,
        out_specs=(P(("blk", "table"), None), P("blk", "table", None, None)),
        check_vma=False,
    )
```

profile of v0, /device:TPU:0, one launch (start us, length us, event | category | flops | bytes accessed | tf_op | source)
XLA Modules:
  0.0 134.0 jit_solution(799297158164035277)
XLA Ops:
  0.6 1.4 %fusion.62 = s32[26,28]{0,1:T(8,128)} fusion(s32[26]{0:T(128)} %param.14), kind=kLoop, calls=%fused_computation.124 | loop fusion | flops 1456 | bytes 3016 | tf_op jit(solution)/shard_map/convert_element_type | solution.py:41
  2.1 0.8 copy.51
  2.9 1.5 %multiply_reduce_fusion = s32[128,28]{0,1:T(8,128)} fusion(s32[26,28]{1,0:T(8,128)S(1)} %copy.51, s32[128,26]{0,1:T(8,128)} %param.13), kind=kLoop, calls=%fused_computation.68 | loop fusion | flops 182784 | bytes 30560 | tf_op jit(solution)/shard_map/reduce_sum | solution.py:42
  4.4 0.7 reshape.50
  5.1 7.9 %all_to_all.15 = s32[128,4,7]{0,2,1:T(8,128)S(1)} all-to-all(s32[128,4,7]{0,2,1:T(8,128)S(1)} %reshape.50), channel_id=1, replica_groups=mesh['blk'=8,'table'=4] {'table'}, dimensions={1} | all-to-all | bytes 28672 | tf_op jit(solution)/shard_map/all_to_all | solution.py:45
  13.0 0.6 fusion.69
  13.6 1.4 %copy.58 = s32[128,4,1]{1,0,2:T(8,128)} copy(s32[128,4,1]{0,2,1:T(1,128)} %get-tuple-element.9) | data formatting | bytes 4096 | tf_op jit(solution)/shard_map/slice | solution.py:51
  15.0 1.5 %eq.366 = s32[512]{0:T(512)} reshape(s32[128,4,1]{1,0,2:T(8,128)} %copy.58) | data formatting | bytes 4096 | tf_op jit(solution)/shard_map/eq | solution.py:52
  16.5 1.4 %copy.57 = s32[128,4,1]{1,0,2:T(8,128)} copy(s32[128,4,1]{0,2,1:T(1,128)} %get-tuple-element.10) | data formatting | bytes 4096 | tf_op jit(solution)/shard_map/slice | solution.py:51
  17.9 1.5 %eq.363 = s32[512]{0:T(512)} reshape(s32[128,4,1]{1,0,2:T(8,128)} %copy.57) | data formatting | bytes 4096 | tf_op jit(solution)/shard_map/eq | solution.py:52
  19.5 1.4 %copy.56 = s32[128,4,1]{1,0,2:T(8,128)} copy(s32[128,4,1]{0,2,1:T(1,128)} %get-tuple-element.11) | data formatting | bytes 4096 | tf_op jit(solution)/shard_map/slice | solution.py:51
  20.9 1.5 %eq.360 = s32[512]{0:T(512)} reshape(s32[128,4,1]{1,0,2:T(8,128)} %copy.56) | data formatting | bytes 4096 | tf_op jit(solution)/shard_map/eq | solution.py:52
  22.4 0.7 copy.55
  23.1 1.5 %eq.357 = s32[512]{0:T(512)} reshape(s32[128,4,1]{1,0,2:T(8,128)} %copy.55) | data formatting | bytes 4096 | tf_op jit(solution)/shard_map/eq | solution.py:52
  24.7 0.7 copy.54
  25.4 1.5 %eq.354 = s32[512]{0:T(512)} reshape(s32[128,4,1]{1,0,2:T(8,128)} %copy.54) | data formatting | bytes 4096 | tf_op jit(solution)/shard_map/eq | solution.py:52
  26.9 0.7 copy.53
  27.7 0.9 eq.351
  28.6 0.7 copy.52
  29.4 1.5 %eq.348 = s32[512]{0:T(512)} reshape(s32[128,4,1]{1,0,2:T(8,128)} %copy.52) | data formatting | bytes 4096 | tf_op jit(solution)/shard_map/eq | solution.py:52
  30.9 1.3 convolution_convert_fusion.10
  32.2 1.3 convolution_convert_fusion.9
  33.4 1.3 convolution_convert_fusion.8
  34.7 1.3 convolution_convert_fusion.7
  36.0 1.3 convolution_convert_fusion.6
  37.3 1.3 convolution_convert_fusion.5
  38.6 1.3 convolution_convert_fusion.4
  39.8 0.7 copy_dynamic-update-slice_fusion.6
  40.5 0.7 copy_dynamic-update-slice_fusion.5
  41.2 0.7 copy_dynamic-update-slice_fusion.4
  41.9 0.7 copy_dynamic-update-slice_fusion.3
  42.5 0.7 copy_dynamic-update-slice_fusion.2
  43.2 0.7 copy_dynamic-update-slice_fusion.1
  43.9 0.7 copy_dynamic-update-slice_fusion
  44.6 4.2 %all-to-all-start.1 = ((bf16[128,4,7,128]{3,0,2,1:T(8,128)(2,1)}), bf16[128,4,7,128]{3,0,2,1:T(8,128)(2,1)}, u32[]{:S(2)}, u32[]{:S(2)}) async-start(bf16[128,4,7,128]{3,0,2,1:T(8,128)(2,1)} %copy_dynamic-update-slice_fusion), calls=%async_computation.1 | async-start | bytes 1835008 | tf_op jit(solution)/shard_map/all_to_all | solution.py:58
  48.8 1.5 %copy.50 = bf16[128,128]{0,1:T(8,128)(2,1)} copy(bf16[128,128]{1,0:T(8,128)(2,1)} %param.12) | data formatting | bytes 65536 | tf_op args[2]
  50.3 30.9 %all_gather.3 = bf16[128,128]{1,0:T(8,128)(2,1)S(1)} all-gather(bf16[16,128]{1,0:T(8,128)(2,1)S(1)} %copy-done.6), channel_id=1, replica_groups=mesh['blk'=8,'table'=4] {'blk'}, dimensions={0}, use_global_device_ids=true | all-gather | bytes 36864 | tf_op jit(solution)/shard_map/all_gather | solution.py:35
  81.2 1.9 %fusion.13 = bf16[128,1,128]{0,2,1:T(8,128)(2,1)} fusion(bf16[128,128]{1,0:T(8,128)(2,1)S(1)} %all_gather.3, bf16[128,128]{0,1:T(8,128)(2,1)} %copy.50, s32[128]{0:T(128)S(1)} %get-tuple-element.30, s32[128]{0:T(128)S(1)} %get-tuple-element.31, s32[128]{0:T(128)S(1)} %get-tuple-element.17, s32[128]{0:T(128)S(1)} %get-tuple-element.18, ...), kind=kOutput, calls=%fused_computation.37 | convolution fusion | flops 5029888 | bytes 106496 | tf_op jit(solution)/shard_map/dot_general | solution.py:37
  83.1 1.5 %copy.68 = bf16[128,1,128]{2,1,0:T(2,128)(2,1)} copy(bf16[128,1,128]{0,2,1:T(8,128)(2,1)} %fusion.13) | data formatting | bytes 65536 | tf_op jit(solution)/shard_map/broadcast_in_dim | solution.py:67
  84.6 1.9 %fusion.3 = bf16[128,26,128]{2,1,0:T(8,128)(2,1)S(1)} fusion(bf16[128,28,128]{2,0,1:T(8,128)(2,1)} %bitcast.32, s32[26]{0:T(128)S(1)} %copy-done.4), kind=kOutput, calls=%fused_computation.10 | convolution fusion | flops 24283272 | bytes 1769576 | tf_op jit(solution)/shard_map/skd,tk->std/dot_general | solution.py:60
  86.5 1.5 %pad_maximum_fusion = bf16[128,27,128]{2,1,0:T(8,128)(2,1)} fusion(bf16[128,26,128]{2,1,0:T(8,128)(2,1)S(1)} %fusion.3, bf16[128,1,128]{2,1,0:T(2,128)(2,1)S(1)} %copy-done.1), kind=kLoop, calls=%fused_computation.38 | loop fusion | flops 1769472 | bytes 1769472 | tf_op jit(solution)/shard_map/concatenate | solution.py:67
  88.0 2.6 %copy.69 = bf16[128,27,128]{0,2,1:T(8,128)(2,1)} copy(bf16[128,27,128]{2,1,0:T(8,128)(2,1)} %pad_maximum_fusion) | data formatting | bytes 1769472 | tf_op jit(solution)/shard_map/concatenate | solution.py:67
  90.6 2.2 %copy.70 = bf16[128,3456]{1,0:T(8,128)(2,1)} copy(bf16[128,3456]{0,1:T(8,128)(2,1)} %bitcast.142) | data formatting | bytes 1769472 | tf_op jit(solution)/shard_map/reshape | solution.py:67
  92.9 5.3 %fusion.2 = (bf16[128,3456]{1,0:T(8,128)(2,1)}, f32[128,3456]{1,0:T(8,128)}) fusion(bf16[128,3456]{1,0:T(8,128)(2,1)} %copy.70, f32[3456]{0:T(1024)S(1)} %copy-done.2, bf16[512,3456]{1,0:T(8,128)(2,1)S(1)} %copy-done, bf16[128,3456]{0,1:T(8,128)(2,1)} %bitcast.143, bf16[3456,512]{1,0:T(8,128)(2,1)} %param.16), kind=kOutput, calls=%fused_computation.7 | convolution fusion | flops 908247040 | bytes 11515392 | tf_op jit(solution)/shard_map/dot_general | solution.py:71
  98.2 6.3 %fusion = bf16[128,3456]{1,0:T(8,128)(2,1)} fusion(bf16[3456,512]{1,0:T(8,128)(2,1)} %param.16, bf16[128,3456]{1,0:T(8,128)(2,1)} %param.19, f32[128,3456]{1,0:T(8,128)} %get-tuple-element.33, bf16[512,3456]{1,0:T(8,128)(2,1)S(1)} %copy-done, bf16[128,3456]{1,0:T(8,128)(2,1)} %copy.70), kind=kOutput, calls=%fused_computation.2 | convolution fusion | flops 910016512 | bytes 11501568 | tf_op jit(solution)/shard_map/dot_general | solution.py:77
  104.5 2.2 %copy.71 = bf16[128,3456]{0,1:T(8,128)(2,1)} copy(bf16[128,3456]{1,0:T(8,128)(2,1)} %fusion) | data formatting | bytes 1769472 | tf_op jit(solution)/shard_map/convert_element_type | solution.py:80
  106.7 2.2 %slice.166 = bf16[128,26,128]{0,2,1:T(8,128)(2,1)} slice(bf16[128,27,128]{0,2,1:T(8,128)(2,1)} %bitcast.145), slice={[0:128], [1:27], [0:128]} | slice | bytes 1703936 | tf_op jit(solution)/shard_map/slice | solution.py:81
  108.9 2.6 %copy.83 = bf16[128,26,128]{2,1,0:T(8,128)(2,1)} copy(bf16[128,26,128]{0,2,1:T(8,128)(2,1)} %slice.166) | data formatting | bytes 1703936
  111.5 1.6 %fusion.4 = bf16[128,28,128]{2,1,0:T(8,128)(2,1)S(1)} fusion(bf16[128,26,128]{2,1,0:T(8,128)(2,1)} %copy.83, s32[26]{0:T(128)S(1)} %copy-done.5), kind=kOutput, calls=%fused_computation.11 | convolution fusion | flops 24316040 | bytes 1769576 | tf_op jit(solution)/shard_map/std,tk->skd/dot_general | solution.py:82
  113.1 0.4 copy.73
  113.5 16.1 %all_to_all.16 = bf16[128,4,7,128]{3,0,2,1:T(8,128)(2,1)S(1)} all-to-all(bf16[128,4,7,128]{3,0,2,1:T(8,128)(2,1)S(1)} %bitcast.144), channel_id=1, replica_groups=mesh['blk'=8,'table'=4] {'table'}, dimensions={1} | all-to-all | bytes 1835008 | tf_op jit(solution)/shard_map/all_to_all | solution.py:84
  129.7 0.1 copy.80
  129.8 0.1 copy.79
  129.9 0.1 copy.78
  130.0 0.1 copy.77
  130.2 0.1 copy.76
  130.5 0.3 fusion.11
  130.9 0.3 fusion.10
  131.2 0.3 fusion.9
  131.5 0.3 fusion.8
  131.8 0.3 fusion.7
  132.1 0.3 fusion.6
  132.4 0.3 fusion.5
  132.8 1.2 copy-done.18
  (42 shorter events, 0.4 us)
Async XLA Ops:
  0.6 92.2 %copy-start = (bf16[512,3456]{1,0:T(8,128)(2,1)S(1)}, bf16[512,3456]{1,0:T(8,128)(2,1)}, u32[]{:S(2)}) copy-start(bf16[512,3456]{1,0:T(8,128)(2,1)} %param.17) | copy-start | bytes 10616836
  23.1 12.9 %copy-start.10 = (s32[512]{0:T(512)S(1)}, s32[512]{0:T(512)}, u32[]{:S(2)}) copy-start(s32[512]{0:T(512)} %eq.360) | copy-start | bytes 6148
  25.4 9.3 %copy-start.12 = (s32[512]{0:T(512)S(1)}, s32[512]{0:T(512)}, u32[]{:S(2)}) copy-start(s32[512]{0:T(512)} %eq.357) | copy-start | bytes 6148
  28.6 9.9 %copy-start.15 = (s32[512]{0:T(512)}, s32[512]{0:T(512)S(1)}, u32[]{:S(2)}) copy-start(s32[512]{0:T(512)S(1)} %eq.351) | copy-start | bytes 6148
  29.4 9.2 %copy-start.7 = (s32[512]{0:T(512)S(1)}, s32[512]{0:T(512)}, u32[]{:S(2)}) copy-start(s32[512]{0:T(512)} %eq.366) | copy-start | bytes 6148
  39.8 10.5 %copy-start.6 = (bf16[16,128]{1,0:T(8,128)(2,1)S(1)}, bf16[16,128]{1,0:T(8,128)(2,1)}, u32[]{:S(2)}) copy-start(bf16[16,128]{1,0:T(8,128)(2,1)} %param.10) | copy-start | bytes 12292
  39.8 41.4 %copy-start.3 = (s32[128,16]{0,1:T(8,128)S(1)}, s32[128,16]{0,1:T(8,128)}, u32[]{:S(2)}) copy-start(s32[128,16]{0,1:T(8,128)} %param.11) | copy-start | bytes 24580
  43.2 41.4 %copy-start.4 = (s32[26]{0:T(128)S(1)}, s32[26]{0:T(128)}, u32[]{:S(2)}) copy-start(s32[26]{0:T(128)} %param.14) | copy-start | bytes 316
  44.6 40.0 %all-to-all-start.1 = ((bf16[128,4,7,128]{3,0,2,1:T(8,128)(2,1)}), bf16[128,4,7,128]{3,0,2,1:T(8,128)(2,1)}, u32[]{:S(2)}, u32[]{:S(2)}) async-start(bf16[128,4,7,128]{3,0,2,1:T(8,128)(2,1)} %copy_dynamic-update-slice_fusion), calls=%async_computation.1 | async-start | bytes 1835008 | tf_op jit(solution)/shard_map/all_to_all | solution.py:58
  84.6 1.9 %copy-start.1 = (bf16[128,1,128]{2,1,0:T(2,128)(2,1)S(1)}, bf16[128,1,128]{2,1,0:T(2,128)(2,1)}, u32[]{:S(2)}) copy-start(bf16[128,1,128]{2,1,0:T(2,128)(2,1)} %copy.68) | copy-start | bytes 98308
  88.0 4.8 %copy-start.2 = (f32[3456]{0:T(1024)S(1)}, f32[3456]{0:T(1024)}, u32[]{:S(2)}) copy-start(f32[3456]{0:T(1024)} %param.18) | copy-start | bytes 41476
  106.7 4.8 %copy-start.5 = (s32[26]{0:T(128)S(1)}, s32[26]{0:T(128)}, u32[]{:S(2)}) copy-start(s32[26]{0:T(128)} %param.14) | copy-start | bytes 316
  129.6 0.9 copy-start.17
  129.6 1.3 copy-start.16
  129.7 1.5 %copy-start.14 = (s32[512]{0:T(512)S(1)}, s32[512]{0:T(512)}, u32[]{:S(2)}) copy-start(s32[512]{0:T(512)} %eq.354) | copy-start | bytes 6148
  129.7 1.8 %copy-start.13 = (s32[512]{0:T(512)S(1)}, s32[512]{0:T(512)}, u32[]{:S(2)}) copy-start(s32[512]{0:T(512)} %eq.357) | copy-start | bytes 6148
  129.9 1.9 %copy-start.11 = (s32[512]{0:T(512)S(1)}, s32[512]{0:T(512)}, u32[]{:S(2)}) copy-start(s32[512]{0:T(512)} %eq.360) | copy-start | bytes 6148
  130.2 2.0 %copy-start.9 = (s32[512]{0:T(512)S(1)}, s32[512]{0:T(512)}, u32[]{:S(2)}) copy-start(s32[512]{0:T(512)} %eq.363) | copy-start | bytes 6148
  130.4 2.0 %copy-start.8 = (s32[512]{0:T(512)S(1)}, s32[512]{0:T(512)}, u32[]{:S(2)}) copy-start(s32[512]{0:T(512)} %eq.366) | copy-start | bytes 6148
  132.8 1.2 copy-start.18
where the time goes:
time: 135 us; the launch traced here: 134 us
  blocking collectives  54.9 us (41%)
  local copies, waits for them, and re-layouts  41.4 us (31%)
  matrix products  28 us (21%)
  other arithmetic  4.39 us (3%)
  starting transfers between devices  4.22 us (3%)
    all_gather x1, blocking collectives, on_device(): block_rows = lax.all_gather(hot_slab, 'blk', axis=0, tiled=True)  30.9 us
    all_to_all x1, blocking collectives, on_device(): lax.all_to_all(grad_slots, 'table', split_axis=1, concat_axis=1, tiled=True)  16.1 us
    eq x7, local copies, waits for them, and re-layouts, on_device(): lookup_selector = (lookup_slot_ids == columns).astype(jnp.bfloat16)  10.1 us
    unnamed x46, local copies, waits for them, and re-layouts  9.46 us
    dot_general x7, matrix products, on_device(): jnp.dot(lookup_selector, cold_tables[lookup_slot_index], preferred_elemen...  8.85 us
    all_to_all x1, blocking collectives, on_device(): lax.all_to_all(send_ids, 'table', split_axis=1, concat_axis=1, tiled=True)  7.91 us
    slice x8, local copies, waits for them, and re-layouts, on_device(): lookup_slot_ids = ids_block[:, :, lookup_slot_index].reshape(row_count, 1)  7.77 us
    dot_general x1, matrix products, on_device(): jnp.dot(grad_low, down_rank.T, preferred_element_type=jnp.float32)  6.33 us
  transfers between devices with their start and end apart: 1, of which 0 were waited for; matrix products, arithmetic and copies ran while one was open for 4% of the time, Pallas kernels for 0%

commit v1 on v0

--- a/solution.py
+++ b/solution.py
@@ -32,7 +32,14 @@
     slots = cold_tables.shape[0]
     table_rows = cold_tables.shape[1]
     slot_total = owners * slots
-    block_rows = lax.all_gather(hot_slab, "blk", axis=0, tiled=True)
+    ways, here = (lax.axis_size("blk"), lax.axis_index("blk"))
+    block_rows, reach = (hot_slab, 1)
+    while reach < ways:
+        theirs = lax.ppermute(block_rows, "blk", [(d, d ^ reach) for d in range(ways)])
+        mine_first = jnp.concatenate([block_rows, theirs], axis=0)
+        theirs_first = jnp.concatenate([theirs, block_rows], axis=0)
+        block_rows = jnp.where(here & reach == 0, mine_first, theirs_first)
+        reach = 2 * reach
     counts = bag_counts(hot_ids, block_rows.shape[0])
     pooled = jnp.dot(counts, block_rows, preferred_element_type=jnp.float32)
     front_row = (dense.astype(jnp.float32) + pooled).astype(jnp.bfloat16)

time: 135 us -> 118 us (0.87)
  blocking collectives: 54.9 us -> 23.9 us
  starting transfers between devices: 4.22 us -> 9.94 us
  waiting for transfers between devices: 0.01 us -> 4.66 us
  other arithmetic: 4.39 us -> 6.54 us
    all_gather x1 -> x0, blocking collectives: 30.9 us -> none  [on_device(): block_rows = lax.all_gather(hot_slab, 'blk', axis=0, tiled=True)]
    ppermute x0 -> x3, starting transfers between devices: none -> 5.72 us  [on_device(): lax.ppermute(block_rows, 'blk', [(d, d ^ reach) for d in range(ways)])]
    ppermute x0 -> x3, waiting for transfers between devices: none -> 4.66 us  [on_device(): lax.ppermute(block_rows, 'blk', [(d, d ^ reach) for d in range(ways)])]
    select_n x0 -> x2, other arithmetic: none -> 2.15 us  [on_device(): block_rows = jnp.where(here & reach == 0, mine_first, theirs_first)]
    unnamed x46 -> x44, local copies, waits for them, and re-layouts: 9.46 us -> 9.46 us
  transfers between devices with their start and end apart: 1 -> 4, of which waited for: 0 -> 3; matrix products, arithmetic and copies ran while one was open for 4% -> 7% of each run, Pallas kernels for 0% -> 0%
where the time goes in v1:
time: 118 us; the launch traced here: 116 us
  local copies, waits for them, and re-layouts  42.1 us (36%)
  matrix products  28.1 us (24%)
  blocking collectives  23.9 us (20%)
  starting transfers between devices  9.94 us (8%)
  other arithmetic  6.54 us (6%)
  waiting for transfers between devices  4.66 us (4%)
    all_to_all x1, blocking collectives, on_device(): lax.all_to_all(grad_slots, 'table', split_axis=1, concat_axis=1, tiled=True)  16 us
    eq x7, local copies, waits for them, and re-layouts, on_device(): lookup_selector = (lookup_slot_ids == columns).astype(jnp.bfloat16)  10.1 us
    unnamed x44, local copies, waits for them, and re-layouts  9.46 us
    dot_general x7, matrix products, on_device(): jnp.dot(lookup_selector, cold_tables[lookup_slot_index], preferred_elemen...  8.85 us
    all_to_all x1, blocking collectives, on_device(): lax.all_to_all(send_ids, 'table', split_axis=1, concat_axis=1, tiled=True)  7.91 us
    slice x8, local copies, waits for them, and re-layouts, on_device(): lookup_slot_ids = ids_block[:, :, lookup_slot_index].reshape(row_count, 1)  7.78 us
    dot_general x1, matrix products, on_device(): jnp.dot(grad_low, down_rank.T, preferred_element_type=jnp.float32)  6.31 us
    ppermute x3, starting transfers between devices, on_device(): lax.ppermute(block_rows, 'blk', [(d, d ^ reach) for d in range(ways)])  5.72 us
  transfers between devices with their start and end apart: 4, of which 3 were waited for; matrix products, arithmetic and copies ran while one was open for 7% of the time, Pallas kernels for 0%

profile of v1, /device:TPU:0, one launch (start us, length us, event | category | flops | bytes accessed | tf_op | source)
XLA Modules:
  0.0 116.3 jit_solution(8942580780831170309)
XLA Ops:
  0.6 1.4 %fusion.68 = s32[26,28]{0,1:T(8,128)} fusion(s32[26]{0:T(128)} %param.14), kind=kLoop, calls=%fused_computation.132 | loop fusion | flops 1456 | bytes 3016 | tf_op jit(solution)/shard_map/convert_element_type | solution.py:48
  2.1 0.8 copy.51
  2.9 1.5 %multiply_reduce_fusion = s32[128,28]{0,1:T(8,128)} fusion(s32[26,28]{1,0:T(8,128)S(1)} %copy.51, s32[128,26]{0,1:T(8,128)} %param.13), kind=kLoop, calls=%fused_computation.68 | loop fusion | flops 182784 | bytes 30560 | tf_op jit(solution)/shard_map/reduce_sum | solution.py:49
  4.4 0.7 reshape.50
  5.1 7.9 %all_to_all.15 = s32[128,4,7]{0,2,1:T(8,128)S(1)} all-to-all(s32[128,4,7]{0,2,1:T(8,128)S(1)} %reshape.50), channel_id=1, replica_groups=mesh['blk'=8,'table'=4] {'table'}, dimensions={1} | all-to-all | bytes 28672 | tf_op jit(solution)/shard_map/all_to_all | solution.py:52
  13.0 0.6 fusion.76
  13.6 1.4 %copy.58 = s32[128,4,1]{1,0,2:T(8,128)} copy(s32[128,4,1]{0,2,1:T(1,128)} %get-tuple-element.9) | data formatting | bytes 4096 | tf_op jit(solution)/shard_map/slice | solution.py:58
  15.0 1.5 %eq.378 = s32[512]{0:T(512)} reshape(s32[128,4,1]{1,0,2:T(8,128)} %copy.58) | data formatting | bytes 4096 | tf_op jit(solution)/shard_map/eq | solution.py:59
  16.5 1.4 %copy.57 = s32[128,4,1]{1,0,2:T(8,128)} copy(s32[128,4,1]{0,2,1:T(1,128)} %get-tuple-element.10) | data formatting | bytes 4096 | tf_op jit(solution)/shard_map/slice | solution.py:58
  17.9 1.5 %eq.375 = s32[512]{0:T(512)} reshape(s32[128,4,1]{1,0,2:T(8,128)} %copy.57) | data formatting | bytes 4096 | tf_op jit(solution)/shard_map/eq | solution.py:59
  19.5 1.4 %copy.56 = s32[128,4,1]{1,0,2:T(8,128)} copy(s32[128,4,1]{0,2,1:T(1,128)} %get-tuple-element.11) | data formatting | bytes 4096 | tf_op jit(solution)/shard_map/slice | solution.py:58
  20.9 1.5 %eq.372 = s32[512]{0:T(512)} reshape(s32[128,4,1]{1,0,2:T(8,128)} %copy.56) | data formatting | bytes 4096 | tf_op jit(solution)/shard_map/eq | solution.py:59
  22.4 0.7 copy.55
  23.1 1.5 %eq.369 = s32[512]{0:T(512)} reshape(s32[128,4,1]{1,0,2:T(8,128)} %copy.55) | data formatting | bytes 4096 | tf_op jit(solution)/shard_map/eq | solution.py:59
  24.7 0.7 copy.54
  25.4 1.5 %eq.366 = s32[512]{0:T(512)} reshape(s32[128,4,1]{1,0,2:T(8,128)} %copy.54) | data formatting | bytes 4096 | tf_op jit(solution)/shard_map/eq | solution.py:59
  27.0 0.7 copy.53
  27.7 0.9 eq.363
  28.6 0.7 copy.52
  29.4 1.5 %eq.360 = s32[512]{0:T(512)} reshape(s32[128,4,1]{1,0,2:T(8,128)} %copy.52) | data formatting | bytes 4096 | tf_op jit(solution)/shard_map/eq | solution.py:59
  30.9 1.3 %convolution_convert_fusion.10 = bf16[512,128]{1,0:T(8,128)(2,1)S(1)} fusion(s32[512]{0:T(512)} %eq.360, bf16[7,512,128]{2,1,0:T(8,128)(2,1)} %param.15), kind=kOutput, calls=%fused_computation.34 | convolution fusion | flops 67436544 | bytes 264192 | tf_op jit(solution)/shard_map/dot_general | solution.py:60
  32.2 1.3 %convolution_convert_fusion.9 = bf16[512,128]{1,0:T(8,128)(2,1)S(1)} fusion(s32[512]{0:T(512)S(1)} %eq.363, bf16[7,512,128]{2,1,0:T(8,128)(2,1)} %param.15), kind=kOutput, calls=%fused_computation.33 | convolution fusion | flops 67436544 | bytes 264192 | tf_op jit(solution)/shard_map/dot_general | solution.py:60
  33.5 1.3 %convolution_convert_fusion.8 = bf16[512,128]{1,0:T(8,128)(2,1)S(1)} fusion(s32[512]{0:T(512)} %eq.366, bf16[7,512,128]{2,1,0:T(8,128)(2,1)} %param.15), kind=kOutput, calls=%fused_computation.32 | convolution fusion | flops 67436544 | bytes 264192 | tf_op jit(solution)/shard_map/dot_general | solution.py:60
  34.7 1.3 %convolution_convert_fusion.7 = bf16[512,128]{1,0:T(8,128)(2,1)S(1)} fusion(s32[512]{0:T(512)S(1)} %copy-done.11, bf16[7,512,128]{2,1,0:T(8,128)(2,1)} %param.15), kind=kOutput, calls=%fused_computation.31 | convolution fusion | flops 67436544 | bytes 264192 | tf_op jit(solution)/shard_map/dot_general | solution.py:60
  36.0 1.3 %convolution_convert_fusion.6 = bf16[512,128]{1,0:T(8,128)(2,1)S(1)} fusion(s32[512]{0:T(512)S(1)} %copy-done.9, bf16[7,512,128]{2,1,0:T(8,128)(2,1)} %param.15), kind=kOutput, calls=%fused_computation.30 | convolution fusion | flops 67436544 | bytes 264192 | tf_op jit(solution)/shard_map/dot_general | solution.py:60
  37.3 1.3 %convolution_convert_fusion.5 = bf16[512,128]{1,0:T(8,128)(2,1)S(1)} fusion(s32[512]{0:T(512)} %eq.375, bf16[7,512,128]{2,1,0:T(8,128)(2,1)} %param.15), kind=kOutput, calls=%fused_computation.29 | convolution fusion | flops 67436544 | bytes 264192 | tf_op jit(solution)/shard_map/dot_general | solution.py:60
  38.6 1.3 %convolution_convert_fusion.4 = bf16[512,128]{1,0:T(8,128)(2,1)S(1)} fusion(s32[512]{0:T(512)S(1)} %copy-done.6, bf16[7,512,128]{2,1,0:T(8,128)(2,1)} %param.15), kind=kOutput, calls=%fused_computation.28 | convolution fusion | flops 67436544 | bytes 264192 | tf_op jit(solution)/shard_map/dot_general | solution.py:60
  39.9 0.7 copy_dynamic-update-slice_fusion.6
  40.5 0.7 copy_dynamic-update-slice_fusion.5
  41.2 0.7 copy_dynamic-update-slice_fusion.4
  41.9 0.7 copy_dynamic-update-slice_fusion.3
  42.6 0.7 copy_dynamic-update-slice_fusion.2
  43.2 0.7 copy_dynamic-update-slice_fusion.1
  43.9 0.7 copy_dynamic-update-slice_fusion
  44.6 4.2 %all-to-all-start.1 = ((bf16[128,4,7,128]{3,0,2,1:T(8,128)(2,1)}), bf16[128,4,7,128]{3,0,2,1:T(8,128)(2,1)}, u32[]{:S(2)}, u32[]{:S(2)}) async-start(bf16[128,4,7,128]{3,0,2,1:T(8,128)(2,1)} %copy_dynamic-update-slice_fusion), calls=%async_computation.1 | async-start | bytes 1835008 | tf_op jit(solution)/shard_map/all_to_all | solution.py:65
  48.8 1.6 %collective-permute-start = (bf16[16,128]{1,0:T(8,128)(2,1)S(1)}, bf16[16,128]{1,0:T(8,128)(2,1)}, u32[]{:S(2)}, u32[]{:S(2)}) collective-permute-start(bf16[16,128]{1,0:T(8,128)(2,1)S(1)} %copy-done.5), channel_id=1, source_target_pairs={{0,4},{4,0},{8,12},{12,8},{16,20},{20,16},{24,28},{28,24},{1,5},{5... | collective-permute-start | bytes 12296 | tf_op jit(solution)/shard_map/ppermute | solution.py:38
  50.4 2.2 %collective-permute-done = bf16[16,128]{1,0:T(8,128)(2,1)} collective-permute-done((bf16[16,128]{1,0:T(8,128)(2,1)S(1)}, bf16[16,128]{1,0:T(8,128)(2,1)}, u32[]{:S(2)}, u32[]{:S(2)}) %collective-permute-start) | collective-permute-done | bytes 4128 | tf_op jit(solution)/shard_map/ppermute | solution.py:38
  52.6 0.8 maximum_select_fusion.3
  53.4 1.6 %collective-permute-start.1 = (bf16[32,128]{1,0:T(8,128)(2,1)S(1)}, bf16[32,128]{1,0:T(8,128)(2,1)}, u32[]{:S(2)}, u32[]{:S(2)}) collective-permute-start(bf16[32,128]{1,0:T(8,128)(2,1)S(1)} %maximum_select_fusion.3), channel_id=1, source_target_pairs={{0,8},{4,12},{8,0},{12,4},{16,24},{20,28},{24,16},{28,20},{1,9},{5... | collective-permute-start | bytes 24584 | tf_op jit(solution)/shard_map/ppermute | solution.py:38
  54.9 2.2 %collective-permute-done.1 = bf16[32,128]{1,0:T(8,128)(2,1)} collective-permute-done((bf16[32,128]{1,0:T(8,128)(2,1)S(1)}, bf16[32,128]{1,0:T(8,128)(2,1)}, u32[]{:S(2)}, u32[]{:S(2)}) %collective-permute-start.1) | collective-permute-done | bytes 8224 | tf_op jit(solution)/shard_map/ppermute | solution.py:38
  57.1 1.4 %maximum_select_fusion.2 = bf16[64,128]{1,0:T(8,128)(2,1)} fusion(bf16[32,128]{1,0:T(8,128)(2,1)} %collective-permute-done.1, bf16[32,128]{1,0:T(8,128)(2,1)S(1)} %maximum_select_fusion.3, pred[]{:T(512)S(6)} %eq.356), kind=kLoop, calls=%fused_computation.130 | loop fusion | flops 73728 | bytes 32769 | tf_op jit(solution)/shard_map/jit(_where)/select_n | solution.py:41
  58.5 2.6 %collective-permute-start.2 = (bf16[64,128]{1,0:T(8,128)(2,1)}, bf16[64,128]{1,0:T(8,128)(2,1)}, u32[]{:S(2)}, u32[]{:S(2)}) collective-permute-start(bf16[64,128]{1,0:T(8,128)(2,1)} %maximum_select_fusion.2), channel_id=1, source_target_pairs={{0,16},{4,20},{8,24},{12,28},{16,0},{20,4},{24,8},{28,12},{1,17},{... | collective-permute-start | bytes 49160 | tf_op jit(solution)/shard_map/ppermute | solution.py:38
  61.1 0.6 slice_bitcast_fusion.15
  61.7 1.5 %copy.50 = bf16[128,128]{0,1:T(8,128)(2,1)} copy(bf16[128,128]{1,0:T(8,128)(2,1)} %param.12) | data formatting | bytes 65536 | tf_op args[2]
  63.5 1.9 %fusion.13 = bf16[128,1,128]{0,2,1:T(8,128)(2,1)} fusion(bf16[128,128]{0,1:T(8,128)(2,1)} %copy.50, bf16[64,128]{1,0:T(8,128)(2,1)} %collective-permute-done.2, bf16[64,128]{1,0:T(8,128)(2,1)} %maximum_select_fusion.2, s32[128]{0:T(128)} %get-tuple-element.30, s32[128]{0:T(128)} %get-tuple-element.31, s32[128]{0:T(128)S(1)} %get-tuple-element.17, ...), kind=kOutput, calls=%fused_computation.37 | convolution fusion | flops 5177344 | bytes 106497 | tf_op jit(solution)/shard_map/dot_general | solution.py:44
  65.4 1.5 %copy.68 = bf16[128,1,128]{2,1,0:T(2,128)(2,1)} copy(bf16[128,1,128]{0,2,1:T(8,128)(2,1)} %fusion.13) | data formatting | bytes 65536 | tf_op jit(solution)/shard_map/broadcast_in_dim | solution.py:74
  66.9 1.9 %fusion.3 = bf16[128,26,128]{2,1,0:T(8,128)(2,1)S(1)} fusion(bf16[128,28,128]{2,0,1:T(8,128)(2,1)} %bitcast.32, s32[26]{0:T(128)} %param.14), kind=kOutput, calls=%fused_computation.10 | convolution fusion | flops 24283272 | bytes 1769576 | tf_op jit(solution)/shard_map/skd,tk->std/dot_general | solution.py:67
  68.9 1.5 %pad_maximum_fusion = bf16[128,27,128]{2,1,0:T(8,128)(2,1)} fusion(bf16[128,26,128]{2,1,0:T(8,128)(2,1)S(1)} %fusion.3, bf16[128,1,128]{2,1,0:T(2,128)(2,1)S(1)} %copy-done.1), kind=kLoop, calls=%fused_computation.38 | loop fusion | flops 1769472 | bytes 1769472 | tf_op jit(solution)/shard_map/concatenate | solution.py:74
  70.3 2.6 %copy.69 = bf16[128,27,128]{0,2,1:T(8,128)(2,1)} copy(bf16[128,27,128]{2,1,0:T(8,128)(2,1)} %pad_maximum_fusion) | data formatting | bytes 1769472 | tf_op jit(solution)/shard_map/concatenate | solution.py:74
  72.9 2.3 %copy.70 = bf16[128,3456]{1,0:T(8,128)(2,1)} copy(bf16[128,3456]{0,1:T(8,128)(2,1)} %bitcast.141) | data formatting | bytes 1769472 | tf_op jit(solution)/shard_map/reshape | solution.py:74
  75.2 5.3 %fusion.2 = (bf16[128,3456]{1,0:T(8,128)(2,1)}, f32[128,3456]{1,0:T(8,128)}) fusion(bf16[128,3456]{1,0:T(8,128)(2,1)} %copy.70, f32[3456]{0:T(1024)S(1)} %copy-done.2, bf16[512,3456]{1,0:T(8,128)(2,1)S(1)} %copy-done, bf16[128,3456]{0,1:T(8,128)(2,1)} %bitcast.142, bf16[3456,512]{1,0:T(8,128)(2,1)} %param.16), kind=kOutput, calls=%fused_computation.7 | convolution fusion | flops 908247040 | bytes 11515392 | tf_op jit(solution)/shard_map/dot_general | solution.py:78
  80.5 6.3 %fusion = bf16[128,3456]{1,0:T(8,128)(2,1)} fusion(bf16[3456,512]{1,0:T(8,128)(2,1)} %param.16, bf16[128,3456]{1,0:T(8,128)(2,1)} %param.19, f32[128,3456]{1,0:T(8,128)} %get-tuple-element.33, bf16[512,3456]{1,0:T(8,128)(2,1)S(1)} %copy-done, bf16[128,3456]{1,0:T(8,128)(2,1)} %copy.70), kind=kOutput, calls=%fused_computation.2 | convolution fusion | flops 910016512 | bytes 11501568 | tf_op jit(solution)/shard_map/dot_general | solution.py:84
  86.8 2.2 %copy.71 = bf16[128,3456]{0,1:T(8,128)(2,1)} copy(bf16[128,3456]{1,0:T(8,128)(2,1)} %fusion) | data formatting | bytes 1769472 | tf_op jit(solution)/shard_map/convert_element_type | solution.py:87
  89.0 2.2 %slice.166 = bf16[128,26,128]{0,2,1:T(8,128)(2,1)} slice(bf16[128,27,128]{0,2,1:T(8,128)(2,1)} %bitcast.144), slice={[0:128], [1:27], [0:128]} | slice | bytes 1703936 | tf_op jit(solution)/shard_map/slice | solution.py:88
  91.2 2.6 %copy.83 = bf16[128,26,128]{2,1,0:T(8,128)(2,1)} copy(bf16[128,26,128]{0,2,1:T(8,128)(2,1)} %slice.166) | data formatting | bytes 1703936
  93.8 1.6 %fusion.4 = bf16[128,28,128]{2,1,0:T(8,128)(2,1)S(1)} fusion(bf16[128,26,128]{2,1,0:T(8,128)(2,1)} %copy.83, s32[26]{0:T(128)S(1)} %copy-done.4), kind=kOutput, calls=%fused_computation.11 | convolution fusion | flops 24316040 | bytes 1769576 | tf_op jit(solution)/shard_map/std,tk->skd/dot_general | solution.py:89
  95.5 0.4 copy.73
  95.8 16.0 %all_to_all.16 = bf16[128,4,7,128]{3,0,2,1:T(8,128)(2,1)S(1)} all-to-all(bf16[128,4,7,128]{3,0,2,1:T(8,128)(2,1)S(1)} %bitcast.143), channel_id=1, replica_groups=mesh['blk'=8,'table'=4] {'table'}, dimensions={1} | all-to-all | bytes 1835008 | tf_op jit(solution)/shard_map/all_to_all | solution.py:91
  112.8 0.3 fusion.11
  113.4 0.3 fusion.9
  113.8 0.3 fusion.8
  114.1 0.3 fusion.7
  114.4 0.3 fusion.6
  115.0 1.2 %copy-done.17 = f32[7,512,128]{2,1,0:T(8,128)} copy-done((f32[7,512,128]{2,1,0:T(8,128)}, f32[7,512,128]{2,1,0:T(8,128)S(1)}, u32[]{:S(2)}) %copy-start.17) | copy-done | bytes 1835032
  (47 shorter events, 1.8 us)
Async XLA Ops:
  0.6 74.6 %copy-start = (bf16[512,3456]{1,0:T(8,128)(2,1)S(1)}, bf16[512,3456]{1,0:T(8,128)(2,1)}, u32[]{:S(2)}) copy-start(bf16[512,3456]{1,0:T(8,128)(2,1)} %param.17) | copy-start | bytes 10616836
  23.1 12.9 %copy-start.9 = (s32[512]{0:T(512)S(1)}, s32[512]{0:T(512)}, u32[]{:S(2)}) copy-start(s32[512]{0:T(512)} %eq.372) | copy-start | bytes 6148
  25.4 9.3 %copy-start.11 = (s32[512]{0:T(512)S(1)}, s32[512]{0:T(512)}, u32[]{:S(2)}) copy-start(s32[512]{0:T(512)} %eq.369) | copy-start | bytes 6148
  28.6 9.9 %copy-start.14 = (s32[512]{0:T(512)}, s32[512]{0:T(512)S(1)}, u32[]{:S(2)}) copy-start(s32[512]{0:T(512)S(1)} %eq.363) | copy-start | bytes 6148
  29.4 9.2 %copy-start.6 = (s32[512]{0:T(512)S(1)}, s32[512]{0:T(512)}, u32[]{:S(2)}) copy-start(s32[512]{0:T(512)} %eq.378) | copy-start | bytes 6148
  39.8 9.0 %copy-start.5 = (bf16[16,128]{1,0:T(8,128)(2,1)S(1)}, bf16[16,128]{1,0:T(8,128)(2,1)}, u32[]{:S(2)}) copy-start(bf16[16,128]{1,0:T(8,128)(2,1)} %param.10) | copy-start | bytes 12292
  39.9 21.2 %copy-start.3 = (s32[128,16]{0,1:T(8,128)S(1)}, s32[128,16]{0,1:T(8,128)}, u32[]{:S(2)}) copy-start(s32[128,16]{0,1:T(8,128)} %param.11) | copy-start | bytes 24580
  44.6 22.3 %all-to-all-start.1 = ((bf16[128,4,7,128]{3,0,2,1:T(8,128)(2,1)}), bf16[128,4,7,128]{3,0,2,1:T(8,128)(2,1)}, u32[]{:S(2)}, u32[]{:S(2)}) async-start(bf16[128,4,7,128]{3,0,2,1:T(8,128)(2,1)} %copy_dynamic-update-slice_fusion), calls=%async_computation.1 | async-start | bytes 1835008 | tf_op jit(solution)/shard_map/all_to_all | solution.py:65
  48.8 3.8 %collective-permute-start = (bf16[16,128]{1,0:T(8,128)(2,1)S(1)}, bf16[16,128]{1,0:T(8,128)(2,1)}, u32[]{:S(2)}, u32[]{:S(2)}) collective-permute-start(bf16[16,128]{1,0:T(8,128)(2,1)S(1)} %copy-done.5), channel_id=1, source_target_pairs={{0,4},{4,0},{8,12},{12,8},{16,20},{20,16},{24,28},{28,24},{1,5},{5... | collective-permute-start | bytes 12296 | tf_op jit(solution)/shard_map/ppermute | solution.py:38
  53.4 3.8 %collective-permute-start.1 = (bf16[32,128]{1,0:T(8,128)(2,1)S(1)}, bf16[32,128]{1,0:T(8,128)(2,1)}, u32[]{:S(2)}, u32[]{:S(2)}) collective-permute-start(bf16[32,128]{1,0:T(8,128)(2,1)S(1)} %maximum_select_fusion.3), channel_id=1, source_target_pairs={{0,8},{4,12},{8,0},{12,4},{16,24},{20,28},{24,16},{28,20},{1,9},{5... | collective-permute-start | bytes 24584 | tf_op jit(solution)/shard_map/ppermute | solution.py:38
  58.5 5.0 %collective-permute-start.2 = (bf16[64,128]{1,0:T(8,128)(2,1)}, bf16[64,128]{1,0:T(8,128)(2,1)}, u32[]{:S(2)}, u32[]{:S(2)}) collective-permute-start(bf16[64,128]{1,0:T(8,128)(2,1)} %maximum_select_fusion.2), channel_id=1, source_target_pairs={{0,16},{4,20},{8,24},{12,28},{16,0},{20,4},{24,8},{28,12},{1,17},{... | collective-permute-start | bytes 49160 | tf_op jit(solution)/shard_map/ppermute | solution.py:38
  66.9 1.9 %copy-start.1 = (bf16[128,1,128]{2,1,0:T(2,128)(2,1)S(1)}, bf16[128,1,128]{2,1,0:T(2,128)(2,1)}, u32[]{:S(2)}) copy-start(bf16[128,1,128]{2,1,0:T(2,128)(2,1)} %copy.68) | copy-start | bytes 98308
  70.3 4.9 %copy-start.2 = (f32[3456]{0:T(1024)S(1)}, f32[3456]{0:T(1024)}, u32[]{:S(2)}) copy-start(f32[3456]{0:T(1024)} %param.18) | copy-start | bytes 41476
  89.0 4.8 %copy-start.4 = (s32[26]{0:T(128)S(1)}, s32[26]{0:T(128)}, u32[]{:S(2)}) copy-start(s32[26]{0:T(128)} %param.14) | copy-start | bytes 316
  111.9 0.9 copy-start.16
  111.9 1.3 %copy-start.15 = (s32[512]{0:T(512)S(1)}, s32[512]{0:T(512)}, u32[]{:S(2)}) copy-start(s32[512]{0:T(512)} %copy-done.14) | copy-start | bytes 6148
  111.9 1.5 %copy-start.13 = (s32[512]{0:T(512)S(1)}, s32[512]{0:T(512)}, u32[]{:S(2)}) copy-start(s32[512]{0:T(512)} %eq.366) | copy-start | bytes 6148
  112.0 1.8 %copy-start.12 = (s32[512]{0:T(512)S(1)}, s32[512]{0:T(512)}, u32[]{:S(2)}) copy-start(s32[512]{0:T(512)} %eq.369) | copy-start | bytes 6148
  112.2 1.9 %copy-start.10 = (s32[512]{0:T(512)S(1)}, s32[512]{0:T(512)}, u32[]{:S(2)}) copy-start(s32[512]{0:T(512)} %eq.372) | copy-start | bytes 6148
  112.4 2.0 %copy-start.8 = (s32[512]{0:T(512)S(1)}, s32[512]{0:T(512)}, u32[]{:S(2)}) copy-start(s32[512]{0:T(512)} %eq.375) | copy-start | bytes 6148
  112.7 2.0 %copy-start.7 = (s32[512]{0:T(512)S(1)}, s32[512]{0:T(512)}, u32[]{:S(2)}) copy-start(s32[512]{0:T(512)} %eq.378) | copy-start | bytes 6148
  115.0 1.2 %copy-start.17 = (f32[7,512,128]{2,1,0:T(8,128)}, f32[7,512,128]{2,1,0:T(8,128)S(1)}, u32[]{:S(2)}) copy-start(f32[7,512,128]{2,1,0:T(8,128)S(1)} %fusion.5) | copy-start | bytes 5505028
